TPU v7x, 128 devices: a whole 4x4x4 slice. The times are simulated.
128 devices in a mesh: width: 4 (over z), row: 4 (over y), src: 8 (over x, core).
Axes of the slice: x: 4, y: 4, z: 4, core: 2. Of those that a mesh axis runs over, the one named last changes fastest.
Arguments:
- query_rows: bfloat16 [1024, 8192], P('row', 'width'), may hold values from -150 to 150
- key_rows: bfloat16 [1024, 1024], P('src', 'width'), may hold values from -7 to 7
- value_rows: bfloat16 [1024, 1024], P('src'), may hold values from -6 to 6
- out_proj: bfloat16 [8192, 8192], P(('row', 'src'), 'width'), may hold values from -0.0625 to 0.0625
Outputs:
- share: float32 [1024, 1024], P('row', ('src', 'width'))
All inputs are finite; a program needn't handle non-finite values.
Results may differ from a plain program's by a relative error of at most 0.0014.
Values may be sent and summed in bfloat16 or wider, within the bound.
A program may use at most 192 MiB of HBM per device.

v0:
```python
import math
import jax
import jax.numpy as jnp
from jax import lax
from jax.sharding import PartitionSpec as P

H = 64
KV = 8
HD = 128


def sent_to_all(shard, axis):
    copies = jnp.broadcast_to(shard, (lax.axis_size(axis), *shard.shape))
    return lax.all_to_all(copies, axis, split_axis=0, concat_axis=0, tiled=True)


def gathered_once(shard, axis):
    leaves = jax.tree.leaves(shard)
    sequence = sorted(range(len(leaves)), key=lambda k: -leaves[k].size)
    width = (1, *leaves[sequence[0]].shape)[-1]
    lines = [
        jnp.pad(leaves[k].reshape(-1), (0, -leaves[k].size % width)).reshape(-1, width)
        for k in sequence
    ]
    both, at, found = (sent_to_all(jnp.concatenate(lines), axis), 0, {})
    for k, line in zip(sequence, lines):
        slab = both[:, at : at + len(line)].reshape(len(both), -1)
        found[k] = slab[:, : leaves[k].size].reshape(-1, *leaves[k].shape)
        at += len(line)
    numbers = iter(range(len(leaves)))
    return jax.tree.map(lambda _: found[next(numbers)], shard)


def combined_pairwise(pieces, combine):
    while len(jax.tree.leaves(pieces)[0]) > 1:
        pieces = jax.vmap(combine)(
            *(jax.tree.map(lambda part: part[side::2], pieces) for side in (0, 1))
        )
    return jax.tree.map(lambda part: part[0], pieces)


def merged(shard, axis, combine):
    pieces = gathered_once(shard, axis)
    return combined_pairwise(pieces, combine)


def cut_along(shard, dim, size):
    dims = shard.shape
    parts = shard.reshape(*dims[:dim], size, dims[dim] // size, *dims[dim + 1 :])
    return jnp.moveaxis(parts, dim, 0)


def sum_at_owner(shard, axis, dim):
    size = lax.axis_size(axis)
    parts = lax.all_to_all(cut_along(shard, dim, size), axis, 0, 0, tiled=True)
    return jnp.sum(parts, axis=0)


def of_everyone(shard, axis):
    return sent_to_all(shard, axis).sum(axis=0)


def combine_stats(first, second):
    peak_one, mass_one = first
    peak_two, mass_two = second
    larger = jnp.maximum(peak_one, peak_two)
    return (larger, mass_one * jnp.exp(peak_one - larger) + mass_two * jnp.exp(peak_two - larger))


def body(query_rows, key_rows, value_rows, out_proj):
    here_row = lax.axis_index("row")
    here_src = lax.axis_index("src")
    row_count = query_rows.shape[0]
    col_count = key_rows.shape[0]
    group_size = H // KV
    row_pos = here_row * row_count + jnp.arange(row_count, dtype=jnp.int32)
    col_pos = here_src * col_count + jnp.arange(col_count, dtype=jnp.int32)
    local_heads = query_rows.shape[1] // HD
    local_kv = key_rows.shape[1] // HD
    queries = query_rows.reshape(row_count, local_kv, group_size, HD)
    key_heads = key_rows.reshape(col_count, local_kv, HD)
    scores = jnp.einsum("ikgd,jkd->kgij", queries, key_heads, preferred_element_type=jnp.float32)
    scores = scores.reshape(local_heads, row_count, col_count) / jnp.sqrt(jnp.float32(HD))
    causal = row_pos[:, None] >= col_pos[None, :]
    masked = jnp.where(causal, scores, jnp.float32(-1e30))
    row_peak = jnp.max(masked, axis=-1)
    row_mass = jnp.sum(jnp.where(causal, jnp.exp(masked - row_peak[..., None]), 0.0), axis=-1)
    row_peak, row_mass = merged((row_peak, row_mass), "src", combine_stats)
    weights = jnp.where(
        causal, jnp.exp(masked - row_peak[..., None]) / row_mass[..., None], 0.0
    ).astype(jnp.bfloat16)
    weights = lax.all_gather(weights, "width", axis=0, tiled=True)
    value_heads = value_rows.reshape(col_count, KV, HD)
    out_cols = out_proj.shape[1]
    proj_heads = out_proj.reshape(-1, HD, out_cols)
    portion = lax.all_gather(proj_heads, ("row", "src"), axis=0, tiled=True)
    head_count = portion.shape[0]
    head_ids = jnp.arange(head_count, dtype=jnp.int32)
    selector = (head_ids[:, None] // group_size == jnp.arange(KV, dtype=jnp.int32)[None, :]).astype(
        jnp.bfloat16
    )
    chosen = jnp.einsum(
        "hk,jkd->jhd", selector, value_heads, preferred_element_type=jnp.float32
    ).astype(jnp.bfloat16)
    images = jnp.einsum("jhd,hde->jhe", chosen, portion, preferred_element_type=jnp.float32).astype(
        jnp.bfloat16
    )
    row_block = math.gcd(row_count, 64)
    col_block = math.gcd(col_count, 32)
    col_steps = col_count // col_block
    turns = row_count // row_block * col_steps

    def tile(turn_index, running):
        row_start = turn_index // col_steps * row_block
        col_start = turn_index % col_steps * col_block
        row_slice = lax.dynamic_slice_in_dim(row_pos, row_start, row_block)
        col_slice = lax.dynamic_slice_in_dim(col_pos, col_start, col_block)

        def compute(unused):
            attend = lax.dynamic_slice(
                weights, (0, row_start, col_start), (H, row_block, col_block)
            )
            source_images = lax.dynamic_slice_in_dim(images, col_start, col_block, 0)
            contrib = jnp.einsum(
                "hij,jhe->ije", attend, source_images, preferred_element_type=jnp.float32
            )
            return jnp.sum(jnp.abs(contrib), axis=-1)

        def skipped(unused):
            return jnp.zeros((row_block, col_block), jnp.float32)

        result = lax.cond(jnp.max(row_slice) >= jnp.min(col_slice), compute, skipped, 0)
        return lax.dynamic_update_slice(running, result, (row_start, col_start))

    partial_value = lax.fori_loop(0, turns, tile, jnp.zeros((row_count, col_count), jnp.float32))
    summed = sum_at_owner(partial_value, "width", 1)
    totals = of_everyone(jnp.sum(summed, axis=1), ("width", "src"))
    position = (here_row * row_count + jnp.arange(row_count, dtype=jnp.int32) + 1).astype(
        jnp.float32
    )
    return position[:, None] * summed / totals[:, None]


def solution(mesh):
    placed = (P("row", "width"), P("src", "width"), P("src", None), P(("row", "src"), "width"))
    return jax.shard_map(
        body, mesh=mesh, in_specs=placed, out_specs=P("row", ("src", "width")), check_vma=False
    )
```

profile of v0, /device:TPU:25, one launch (start us, length us, event | category | flops | bytes accessed | tf_op | source)
XLA Modules:
  0.0 431.4 jit_solution(18067964968503341397)
XLA Ops:
  6.5 1.5 copy.36
  10.0 5.0 %all-to-all-start = ((f32[8,32,256]{2,1,0:T(8,128)}), f32[8,32,256]{2,1,0:T(8,128)S(1)}, u32[]{:S(2)}, u32[]{:S(2)}) async-start(f32[8,32,256]{2,1,0:T(8,128)} %broadcast_in_dim.44), calls=%async_computation | async-start | bytes 524288 | tf_op jit(solution)/shard_map/all_to_all | solution.py:14
  15.1 1.9 copy.27
  16.9 4.5 %all-to-all-done = f32[8,32,256]{2,1,0:T(8,128)S(1)} async-done(((f32[8,32,256]{2,1,0:T(8,128)}), f32[8,32,256]{2,1,0:T(8,128)S(1)}, u32[]{:S(2)}, u32[]{:S(2)}) %all-to-all-start) | async-done | bytes 262176 | tf_op jit(solution)/shard_map/all_to_all | solution.py:14
  21.6 4.1 select_convert_fusion
  27.2 47.7 %all-gather.5.cloned.1.call-done = bf16[64,256,128]{2,1,0:T(8,128)(2,1)} async-done(((bf16[16,256,128]{2,1,0:T(8,128)(2,1)}), bf16[64,256,128]{2,1,0:T(8,128)(2,1)}) %all-gather.5.cloned.1.call-update) | async-done | bytes 4194320 | tf_op jit(solution)/shard_map/all_gather | solution.py:92
  75.0 15.6 %copy.29 = bf16[64,256,128]{0,1,2:T(8,128)(2,1)} copy(bf16[64,256,128]{2,1,0:T(8,128)(2,1)} %all-gather.5.cloned.1.call-done) | data formatting | bytes 8388608 | tf_op jit(solution)/shard_map/while | solution.py:135
  90.6 100.2 %all-gather.3.cloned.1.call-done = bf16[64,128,2048]{2,1,0:T(8,128)(2,1)} async-done(((bf16[2,128,2048]{2,1,0:T(8,128)(2,1)}), bf16[64,128,2048]{2,1,0:T(8,128)(2,1)}) %all-gather.3.cloned.1.call-update) | async-done | bytes 33554448 | tf_op jit(solution)/shard_map/all_gather | solution.py:96
  190.8 24.2 %convert_bitcast_fusion = bf16[128,64,2048]{2,0,1:T(8,128)(2,1)} fusion(bf16[64,128,2048]{2,1,0:T(8,128)(2,1)} %all-gather.3.cloned.1.call-done, bf16[128,64,128]{2,1,0:T(8,128)(2,1)S(1)} %convert_bitcast_fusion.1), kind=kOutput, calls=%fused_computation.7 | convolution fusion | flops 4311744512 | bytes 69206016 | tf_op jit(solution)/shard_map/jhd,hde->jhe/dot_general | solution.py:105
  215.0 30.0 %copy.28 = bf16[128,64,2048]{2,1,0:T(8,128)(2,1)} copy(bf16[128,64,2048]{2,0,1:T(8,128)(2,1)} %convert_bitcast_fusion) | data formatting | bytes 67108864 | tf_op jit(solution)/shard_map/while | solution.py:135
  245.0 156.7 %while.15 = (s32[]{:T(128)}, f32[256,128]{0,1:T(8,128)S(1)}, s32[256]{0:T(256)S(1)}, s32[128]{0:T(128)S(1)}, bf16[128,64,2048]{2,1,0:T(8,128)(2,1)}, /*index=5*/...) while((s32[]{:T(128)}, f32[256,128]{0,1:T(8,128)S(1)}, ...), condition=%wide.region_8.9_spmd, body=%wide.region_2.8_spmd.sunk | while | flops 545257600 | bytes 8939898 | solution.py:135
  245.0 0.8 dynamic-slice_reduce_fusion.4
  247.9 6.0 %conditional.2 = (f32[64,32]{0,1:T(8,128)S(1)}) conditional(s32[]{:T(128)} %convert_element_type.44, () %tuple.54, (s32[]{:T(128)}, bf16[128,64,2048]{2,1,0:T(8,128)(2,1)}, s32[]{:T(128)}, bf16[64,256,128]{0,1,2:T(8,128)(2,1)}) %tuple.55), branch_computations={%region_5.5_spmd, %region_6.7_spmd} | conditional | flops 545257472 | bytes 8922700 | solution.py:132
  247.9 6.0 %abs_reduce_fusion = f32[32,64]{1,0:T(8,128)S(1)} fusion(bf16[128,64,2048]{2,1,0:T(8,128)(2,1)} %get-tuple-element.172, s32[]{:T(128)S(6)} %select_n.76, bf16[64,256,128]{0,1,2:T(8,128)(2,1)} %get-tuple-element.174, s32[]{:T(128)S(6)} %select_n.77), kind=kOutput, calls=%fused_computation | convolution fusion | flops 545257472 | bytes 8922624 | tf_op jit(solution)/shard_map/while/body/eval_jaxpr/cond/branch_1_fun/hij,jhe->ije/dot_general | solution.py:124
  253.9 0.9 dynamic_update_slice.11
  254.8 0.8 dynamic-slice_reduce_fusion.4
  257.7 6.0 %conditional.2 = (f32[64,32]{0,1:T(8,128)S(1)}) conditional(s32[]{:T(128)} %convert_element_type.44, () %tuple.54, (s32[]{:T(128)}, bf16[128,64,2048]{2,1,0:T(8,128)(2,1)}, s32[]{:T(128)}, bf16[64,256,128]{0,1,2:T(8,128)(2,1)}) %tuple.55), branch_computations={%region_5.5_spmd, %region_6.7_spmd} | conditional | flops 545257472 | bytes 8922700 | solution.py:132
  257.7 6.0 %abs_reduce_fusion = f32[32,64]{1,0:T(8,128)S(1)} fusion(bf16[128,64,2048]{2,1,0:T(8,128)(2,1)} %get-tuple-element.172, s32[]{:T(128)S(6)} %select_n.76, bf16[64,256,128]{0,1,2:T(8,128)(2,1)} %get-tuple-element.174, s32[]{:T(128)S(6)} %select_n.77), kind=kOutput, calls=%fused_computation | convolution fusion | flops 545257472 | bytes 8922624 | tf_op jit(solution)/shard_map/while/body/eval_jaxpr/cond/branch_1_fun/hij,jhe->ije/dot_general | solution.py:124
  263.7 0.9 dynamic_update_slice.11
  264.6 0.8 dynamic-slice_reduce_fusion.4
  267.5 6.0 %conditional.2 = (f32[64,32]{0,1:T(8,128)S(1)}) conditional(s32[]{:T(128)} %convert_element_type.44, () %tuple.54, (s32[]{:T(128)}, bf16[128,64,2048]{2,1,0:T(8,128)(2,1)}, s32[]{:T(128)}, bf16[64,256,128]{0,1,2:T(8,128)(2,1)}) %tuple.55), branch_computations={%region_5.5_spmd, %region_6.7_spmd} | conditional | flops 545257472 | bytes 8922700 | solution.py:132
  267.5 6.0 %abs_reduce_fusion = f32[32,64]{1,0:T(8,128)S(1)} fusion(bf16[128,64,2048]{2,1,0:T(8,128)(2,1)} %get-tuple-element.172, s32[]{:T(128)S(6)} %select_n.76, bf16[64,256,128]{0,1,2:T(8,128)(2,1)} %get-tuple-element.174, s32[]{:T(128)S(6)} %select_n.77), kind=kOutput, calls=%fused_computation | convolution fusion | flops 545257472 | bytes 8922624 | tf_op jit(solution)/shard_map/while/body/eval_jaxpr/cond/branch_1_fun/hij,jhe->ije/dot_general | solution.py:124
  273.5 0.9 dynamic_update_slice.11
  274.4 0.8 dynamic-slice_reduce_fusion.4
  277.3 6.0 %conditional.2 = (f32[64,32]{0,1:T(8,128)S(1)}) conditional(s32[]{:T(128)} %convert_element_type.44, () %tuple.54, (s32[]{:T(128)}, bf16[128,64,2048]{2,1,0:T(8,128)(2,1)}, s32[]{:T(128)}, bf16[64,256,128]{0,1,2:T(8,128)(2,1)}) %tuple.55), branch_computations={%region_5.5_spmd, %region_6.7_spmd} | conditional | flops 545257472 | bytes 8922700 | solution.py:132
  277.3 6.0 %abs_reduce_fusion = f32[32,64]{1,0:T(8,128)S(1)} fusion(bf16[128,64,2048]{2,1,0:T(8,128)(2,1)} %get-tuple-element.172, s32[]{:T(128)S(6)} %select_n.76, bf16[64,256,128]{0,1,2:T(8,128)(2,1)} %get-tuple-element.174, s32[]{:T(128)S(6)} %select_n.77), kind=kOutput, calls=%fused_computation | convolution fusion | flops 545257472 | bytes 8922624 | tf_op jit(solution)/shard_map/while/body/eval_jaxpr/cond/branch_1_fun/hij,jhe->ije/dot_general | solution.py:124
  284.0 0.8 dynamic-slice_reduce_fusion.4
  286.9 6.0 %conditional.2 = (f32[64,32]{0,1:T(8,128)S(1)}) conditional(s32[]{:T(128)} %convert_element_type.44, () %tuple.54, (s32[]{:T(128)}, bf16[128,64,2048]{2,1,0:T(8,128)(2,1)}, s32[]{:T(128)}, bf16[64,256,128]{0,1,2:T(8,128)(2,1)}) %tuple.55), branch_computations={%region_5.5_spmd, %region_6.7_spmd} | conditional | flops 545257472 | bytes 8922700 | solution.py:132
  286.9 6.0 %abs_reduce_fusion = f32[32,64]{1,0:T(8,128)S(1)} fusion(bf16[128,64,2048]{2,1,0:T(8,128)(2,1)} %get-tuple-element.172, s32[]{:T(128)S(6)} %select_n.76, bf16[64,256,128]{0,1,2:T(8,128)(2,1)} %get-tuple-element.174, s32[]{:T(128)S(6)} %select_n.77), kind=kOutput, calls=%fused_computation | convolution fusion | flops 545257472 | bytes 8922624 | tf_op jit(solution)/shard_map/while/body/eval_jaxpr/cond/branch_1_fun/hij,jhe->ije/dot_general | solution.py:124
  292.9 1.1 dynamic_update_slice.11
  294.1 0.8 dynamic-slice_reduce_fusion.4
  297.0 6.0 %conditional.2 = (f32[64,32]{0,1:T(8,128)S(1)}) conditional(s32[]{:T(128)} %convert_element_type.44, () %tuple.54, (s32[]{:T(128)}, bf16[128,64,2048]{2,1,0:T(8,128)(2,1)}, s32[]{:T(128)}, bf16[64,256,128]{0,1,2:T(8,128)(2,1)}) %tuple.55), branch_computations={%region_5.5_spmd, %region_6.7_spmd} | conditional | flops 545257472 | bytes 8922700 | solution.py:132
  297.0 6.0 %abs_reduce_fusion = f32[32,64]{1,0:T(8,128)S(1)} fusion(bf16[128,64,2048]{2,1,0:T(8,128)(2,1)} %get-tuple-element.172, s32[]{:T(128)S(6)} %select_n.76, bf16[64,256,128]{0,1,2:T(8,128)(2,1)} %get-tuple-element.174, s32[]{:T(128)S(6)} %select_n.77), kind=kOutput, calls=%fused_computation | convolution fusion | flops 545257472 | bytes 8922624 | tf_op jit(solution)/shard_map/while/body/eval_jaxpr/cond/branch_1_fun/hij,jhe->ije/dot_general | solution.py:124
  303.0 1.1 dynamic_update_slice.11
  304.2 0.8 dynamic-slice_reduce_fusion.4
  307.0 6.0 %conditional.2 = (f32[64,32]{0,1:T(8,128)S(1)}) conditional(s32[]{:T(128)} %convert_element_type.44, () %tuple.54, (s32[]{:T(128)}, bf16[128,64,2048]{2,1,0:T(8,128)(2,1)}, s32[]{:T(128)}, bf16[64,256,128]{0,1,2:T(8,128)(2,1)}) %tuple.55), branch_computations={%region_5.5_spmd, %region_6.7_spmd} | conditional | flops 545257472 | bytes 8922700 | solution.py:132
  307.1 6.0 %abs_reduce_fusion = f32[32,64]{1,0:T(8,128)S(1)} fusion(bf16[128,64,2048]{2,1,0:T(8,128)(2,1)} %get-tuple-element.172, s32[]{:T(128)S(6)} %select_n.76, bf16[64,256,128]{0,1,2:T(8,128)(2,1)} %get-tuple-element.174, s32[]{:T(128)S(6)} %select_n.77), kind=kOutput, calls=%fused_computation | convolution fusion | flops 545257472 | bytes 8922624 | tf_op jit(solution)/shard_map/while/body/eval_jaxpr/cond/branch_1_fun/hij,jhe->ije/dot_general | solution.py:124
  313.1 1.1 dynamic_update_slice.11
  317.1 6.0 %conditional.2 = (f32[64,32]{0,1:T(8,128)S(1)}) conditional(s32[]{:T(128)} %convert_element_type.44, () %tuple.54, (s32[]{:T(128)}, bf16[128,64,2048]{2,1,0:T(8,128)(2,1)}, s32[]{:T(128)}, bf16[64,256,128]{0,1,2:T(8,128)(2,1)}) %tuple.55), branch_computations={%region_5.5_spmd, %region_6.7_spmd} | conditional | flops 545257472 | bytes 8922700 | solution.py:132
  317.1 6.0 %abs_reduce_fusion = f32[32,64]{1,0:T(8,128)S(1)} fusion(bf16[128,64,2048]{2,1,0:T(8,128)(2,1)} %get-tuple-element.172, s32[]{:T(128)S(6)} %select_n.76, bf16[64,256,128]{0,1,2:T(8,128)(2,1)} %get-tuple-element.174, s32[]{:T(128)S(6)} %select_n.77), kind=kOutput, calls=%fused_computation | convolution fusion | flops 545257472 | bytes 8922624 | tf_op jit(solution)/shard_map/while/body/eval_jaxpr/cond/branch_1_fun/hij,jhe->ije/dot_general | solution.py:124
  323.2 0.9 dynamic_update_slice.11
  327.0 6.0 %conditional.2 = (f32[64,32]{0,1:T(8,128)S(1)}) conditional(s32[]{:T(128)} %convert_element_type.44, () %tuple.54, (s32[]{:T(128)}, bf16[128,64,2048]{2,1,0:T(8,128)(2,1)}, s32[]{:T(128)}, bf16[64,256,128]{0,1,2:T(8,128)(2,1)}) %tuple.55), branch_computations={%region_5.5_spmd, %region_6.7_spmd} | conditional | flops 545257472 | bytes 8922700 | solution.py:132
  327.0 6.0 %abs_reduce_fusion = f32[32,64]{1,0:T(8,128)S(1)} fusion(bf16[128,64,2048]{2,1,0:T(8,128)(2,1)} %get-tuple-element.172, s32[]{:T(128)S(6)} %select_n.76, bf16[64,256,128]{0,1,2:T(8,128)(2,1)} %get-tuple-element.174, s32[]{:T(128)S(6)} %select_n.77), kind=kOutput, calls=%fused_computation | convolution fusion | flops 545257472 | bytes 8922624 | tf_op jit(solution)/shard_map/while/body/eval_jaxpr/cond/branch_1_fun/hij,jhe->ije/dot_general | solution.py:124
  336.6 6.0 %conditional.2 = (f32[64,32]{0,1:T(8,128)S(1)}) conditional(s32[]{:T(128)} %convert_element_type.44, () %tuple.54, (s32[]{:T(128)}, bf16[128,64,2048]{2,1,0:T(8,128)(2,1)}, s32[]{:T(128)}, bf16[64,256,128]{0,1,2:T(8,128)(2,1)}) %tuple.55), branch_computations={%region_5.5_spmd, %region_6.7_spmd} | conditional | flops 545257472 | bytes 8922700 | solution.py:132
  336.6 6.0 %abs_reduce_fusion = f32[32,64]{1,0:T(8,128)S(1)} fusion(bf16[128,64,2048]{2,1,0:T(8,128)(2,1)} %get-tuple-element.172, s32[]{:T(128)S(6)} %select_n.76, bf16[64,256,128]{0,1,2:T(8,128)(2,1)} %get-tuple-element.174, s32[]{:T(128)S(6)} %select_n.77), kind=kOutput, calls=%fused_computation | convolution fusion | flops 545257472 | bytes 8922624 | tf_op jit(solution)/shard_map/while/body/eval_jaxpr/cond/branch_1_fun/hij,jhe->ije/dot_general | solution.py:124
  346.2 6.0 %conditional.2 = (f32[64,32]{0,1:T(8,128)S(1)}) conditional(s32[]{:T(128)} %convert_element_type.44, () %tuple.54, (s32[]{:T(128)}, bf16[128,64,2048]{2,1,0:T(8,128)(2,1)}, s32[]{:T(128)}, bf16[64,256,128]{0,1,2:T(8,128)(2,1)}) %tuple.55), branch_computations={%region_5.5_spmd, %region_6.7_spmd} | conditional | flops 545257472 | bytes 8922700 | solution.py:132
  346.2 6.0 %abs_reduce_fusion = f32[32,64]{1,0:T(8,128)S(1)} fusion(bf16[128,64,2048]{2,1,0:T(8,128)(2,1)} %get-tuple-element.172, s32[]{:T(128)S(6)} %select_n.76, bf16[64,256,128]{0,1,2:T(8,128)(2,1)} %get-tuple-element.174, s32[]{:T(128)S(6)} %select_n.77), kind=kOutput, calls=%fused_computation | convolution fusion | flops 545257472 | bytes 8922624 | tf_op jit(solution)/shard_map/while/body/eval_jaxpr/cond/branch_1_fun/hij,jhe->ije/dot_general | solution.py:124
  355.8 6.0 %conditional.2 = (f32[64,32]{0,1:T(8,128)S(1)}) conditional(s32[]{:T(128)} %convert_element_type.44, () %tuple.54, (s32[]{:T(128)}, bf16[128,64,2048]{2,1,0:T(8,128)(2,1)}, s32[]{:T(128)}, bf16[64,256,128]{0,1,2:T(8,128)(2,1)}) %tuple.55), branch_computations={%region_5.5_spmd, %region_6.7_spmd} | conditional | flops 545257472 | bytes 8922700 | solution.py:132
  355.8 6.0 %abs_reduce_fusion = f32[32,64]{1,0:T(8,128)S(1)} fusion(bf16[128,64,2048]{2,1,0:T(8,128)(2,1)} %get-tuple-element.172, s32[]{:T(128)S(6)} %select_n.76, bf16[64,256,128]{0,1,2:T(8,128)(2,1)} %get-tuple-element.174, s32[]{:T(128)S(6)} %select_n.77), kind=kOutput, calls=%fused_computation | convolution fusion | flops 545257472 | bytes 8922624 | tf_op jit(solution)/shard_map/while/body/eval_jaxpr/cond/branch_1_fun/hij,jhe->ije/dot_general | solution.py:124
  365.2 6.0 %conditional.2 = (f32[64,32]{0,1:T(8,128)S(1)}) conditional(s32[]{:T(128)} %convert_element_type.44, () %tuple.54, (s32[]{:T(128)}, bf16[128,64,2048]{2,1,0:T(8,128)(2,1)}, s32[]{:T(128)}, bf16[64,256,128]{0,1,2:T(8,128)(2,1)}) %tuple.55), branch_computations={%region_5.5_spmd, %region_6.7_spmd} | conditional | flops 545257472 | bytes 8922700 | solution.py:132
  365.3 6.0 %abs_reduce_fusion = f32[32,64]{1,0:T(8,128)S(1)} fusion(bf16[128,64,2048]{2,1,0:T(8,128)(2,1)} %get-tuple-element.172, s32[]{:T(128)S(6)} %select_n.76, bf16[64,256,128]{0,1,2:T(8,128)(2,1)} %get-tuple-element.174, s32[]{:T(128)S(6)} %select_n.77), kind=kOutput, calls=%fused_computation | convolution fusion | flops 545257472 | bytes 8922624 | tf_op jit(solution)/shard_map/while/body/eval_jaxpr/cond/branch_1_fun/hij,jhe->ije/dot_general | solution.py:124
  371.3 0.9 dynamic_update_slice.11
  375.1 6.0 %conditional.2 = (f32[64,32]{0,1:T(8,128)S(1)}) conditional(s32[]{:T(128)} %convert_element_type.44, () %tuple.54, (s32[]{:T(128)}, bf16[128,64,2048]{2,1,0:T(8,128)(2,1)}, s32[]{:T(128)}, bf16[64,256,128]{0,1,2:T(8,128)(2,1)}) %tuple.55), branch_computations={%region_5.5_spmd, %region_6.7_spmd} | conditional | flops 545257472 | bytes 8922700 | solution.py:132
  375.1 6.0 %abs_reduce_fusion = f32[32,64]{1,0:T(8,128)S(1)} fusion(bf16[128,64,2048]{2,1,0:T(8,128)(2,1)} %get-tuple-element.172, s32[]{:T(128)S(6)} %select_n.76, bf16[64,256,128]{0,1,2:T(8,128)(2,1)} %get-tuple-element.174, s32[]{:T(128)S(6)} %select_n.77), kind=kOutput, calls=%fused_computation | convolution fusion | flops 545257472 | bytes 8922624 | tf_op jit(solution)/shard_map/while/body/eval_jaxpr/cond/branch_1_fun/hij,jhe->ije/dot_general | solution.py:124
  381.1 0.9 dynamic_update_slice.11
  384.9 6.0 %conditional.2 = (f32[64,32]{0,1:T(8,128)S(1)}) conditional(s32[]{:T(128)} %convert_element_type.44, () %tuple.54, (s32[]{:T(128)}, bf16[128,64,2048]{2,1,0:T(8,128)(2,1)}, s32[]{:T(128)}, bf16[64,256,128]{0,1,2:T(8,128)(2,1)}) %tuple.55), branch_computations={%region_5.5_spmd, %region_6.7_spmd} | conditional | flops 545257472 | bytes 8922700 | solution.py:132
  385.0 6.0 %abs_reduce_fusion = f32[32,64]{1,0:T(8,128)S(1)} fusion(bf16[128,64,2048]{2,1,0:T(8,128)(2,1)} %get-tuple-element.172, s32[]{:T(128)S(6)} %select_n.76, bf16[64,256,128]{0,1,2:T(8,128)(2,1)} %get-tuple-element.174, s32[]{:T(128)S(6)} %select_n.77), kind=kOutput, calls=%fused_computation | convolution fusion | flops 545257472 | bytes 8922624 | tf_op jit(solution)/shard_map/while/body/eval_jaxpr/cond/branch_1_fun/hij,jhe->ije/dot_general | solution.py:124
  391.0 0.9 dynamic_update_slice.11
  394.8 6.0 %conditional.2 = (f32[64,32]{0,1:T(8,128)S(1)}) conditional(s32[]{:T(128)} %convert_element_type.44, () %tuple.54, (s32[]{:T(128)}, bf16[128,64,2048]{2,1,0:T(8,128)(2,1)}, s32[]{:T(128)}, bf16[64,256,128]{0,1,2:T(8,128)(2,1)}) %tuple.55), branch_computations={%region_5.5_spmd, %region_6.7_spmd} | conditional | flops 545257472 | bytes 8922700 | solution.py:132
  394.8 6.0 %abs_reduce_fusion = f32[32,64]{1,0:T(8,128)S(1)} fusion(bf16[128,64,2048]{2,1,0:T(8,128)(2,1)} %get-tuple-element.172, s32[]{:T(128)S(6)} %select_n.76, bf16[64,256,128]{0,1,2:T(8,128)(2,1)} %get-tuple-element.174, s32[]{:T(128)S(6)} %select_n.77), kind=kOutput, calls=%fused_computation | convolution fusion | flops 545257472 | bytes 8922624 | tf_op jit(solution)/shard_map/while/body/eval_jaxpr/cond/branch_1_fun/hij,jhe->ije/dot_general | solution.py:124
  400.8 0.8 dynamic_update_slice.11
  401.7 8.7 %all_to_all.16 = f32[4,256,32]{1,2,0:T(8,128)S(1)} all-to-all(f32[4,256,32]{1,2,0:T(8,128)S(1)} %bitcast.40), channel_id=1, replica_groups=mesh['width'=4,'row'=4,'src'=8] {'width'}, dimensions={0} | all-to-all | bytes 262144 | tf_op jit(solution)/shard_map/all_to_all | solution.py:55
  411.1 5.6 %all-to-all-start.2 = ((f32[32,1,256]{2,1,0:T(1,128)}), f32[32,1,256]{2,1,0:T(1,128)S(1)}, u32[]{:S(2)}, u32[]{:S(2)}) async-start(f32[32,1,256]{2,1,0:T(1,128)} %broadcast_in_dim.46), calls=%async_computation.2 | async-start | bytes 65536 | tf_op jit(solution)/shard_map/all_to_all | solution.py:14
  416.6 7.2 %all-to-all-done.2 = f32[32,1,256]{2,1,0:T(1,128)S(1)} async-done(((f32[32,1,256]{2,1,0:T(1,128)}), f32[32,1,256]{2,1,0:T(1,128)S(1)}, u32[]{:S(2)}, u32[]{:S(2)}) %all-to-all-start.2) | async-done | bytes 32800 | tf_op jit(solution)/shard_map/all_to_all | solution.py:14
  (60 shorter events, 27.4 us)
Async XLA Ops:
  6.5 1.5 copy-start.1
  10.0 11.5 %all-to-all-start = ((f32[8,32,256]{2,1,0:T(8,128)}), f32[8,32,256]{2,1,0:T(8,128)S(1)}, u32[]{:S(2)}, u32[]{:S(2)}) async-start(f32[8,32,256]{2,1,0:T(8,128)} %broadcast_in_dim.44), calls=%async_computation | async-start | bytes 524288 | tf_op jit(solution)/shard_map/all_to_all | solution.py:14
  14.9 60.0 %all-gather.5.cloned.1.call-start = ((), (), s32[]{:S(2)}) async-start(), calls=%async_computation.4 | async-start | bytes 5242880 | tf_op jit(solution)/shard_map/all_gather | solution.py:92
  21.6 4.9 %copy-start = (bf16[128,1024]{1,0:T(8,128)(2,1)S(1)}, bf16[128,1024]{1,0:T(8,128)(2,1)}, u32[]{:S(2)}) copy-start(bf16[128,1024]{1,0:T(8,128)(2,1)} %param.10) | copy-start | bytes 786436
  25.7 165.1 %all-gather.3.cloned.1.call-start = ((), (), s32[]{:S(2)}) async-start(), calls=%async_computation.3 | async-start | bytes 34603008 | tf_op jit(solution)/shard_map/all_gather | solution.py:96
  411.1 12.8 %all-to-all-start.2 = ((f32[32,1,256]{2,1,0:T(1,128)}), f32[32,1,256]{2,1,0:T(1,128)S(1)}, u32[]{:S(2)}, u32[]{:S(2)}) async-start(f32[32,1,256]{2,1,0:T(1,128)} %broadcast_in_dim.46), calls=%async_computation.2 | async-start | bytes 65536 | tf_op jit(solution)/shard_map/all_to_all | solution.py:14
Sparse Core Ops, SparseCore 0:
  25.8 49.1 all-gather.4
  77.2 113.4 all-gather.2
where the time goes:
time: 432 us; the launch traced here: 431 us
  waiting for transfers between devices  160 us (37%)
  matrix products  122 us (28%)
  local copies, waits for them, and re-layouts  64.2 us (15%)
  other arithmetic  30.2 us (7%)
  loops' own time  22.2 us (5%)
  between operations  13.6 us (3%)
  starting transfers between devices  10.8 us (2%)
  blocking collectives  8.75 us (2%)
    all_gather x1, waiting for transfers between devices, body(): portion = lax.all_gather(proj_heads, ('row', 'src'), axis=0, tiled=True)  100 us
    dot_general x16, matrix products, compute(): jnp.einsum('hij,jhe->ije', attend, source_images, preferred_element_type=...  96.1 us
    all_gather x1, waiting for transfers between devices, body(): weights = lax.all_gather(weights, 'width', axis=0, tiled=True)  47.7 us
    while x2, local copies, waits for them, and re-layouts, body(): lax.fori_loop(0, turns, tile, jnp.zeros((row_count, col_count), jnp.float...  45.6 us
    dot_general x1, matrix products, body(): jnp.einsum('jhd,hde->jhe', chosen, portion, preferred_element_type=jnp.fl...  24.2 us
    another operation x1, loops' own time, body(): lax.fori_loop(0, turns, tile, jnp.zeros((row_count, col_count), jnp.float...  21.8 us
    dynamic_update_slice x16, local copies, waits for them, and re-layouts, tile(): return lax.dynamic_update_slice(running, result, (row_start, col_start))  13.7 us
    reduce_max x16, other arithmetic, tile(): jnp.max(row_slice) >= jnp.min(col_slice)  12.5 us
  transfers between devices with their start and end apart: 4, of which 4 were waited for; matrix products, arithmetic and copies ran while one was open for 4% of the time, Pallas kernels for 0%

commit v1 on v0

--- a/solution.py
+++ b/solution.py
@@ -7,6 +7,19 @@
 H = 64
 KV = 8
 HD = 128
+
+
+def gather_around(x, axis, dim):
+    ways = lax.axis_size(axis)
+    up = [(d, (d + 1) % ways) for d in range(ways)]
+    down = [(d, (d - 1) % ways) for d in range(ways)]
+    earlier, later = ([x], [x])
+    for _ in range(ways // 2):
+        earlier.append(lax.ppermute(earlier[-1], axis, up))
+    for _ in range((ways - 1) // 2):
+        later.append(lax.ppermute(later[-1], axis, down))
+    line = jnp.concatenate([*earlier[::-1], *later[1:]], axis=dim)
+    return jnp.roll(line, (lax.axis_index(axis) - ways // 2) * x.shape[dim], axis=dim)
 
 
 def sent_to_all(shard, axis):
@@ -89,7 +102,7 @@
     weights = jnp.where(
         causal, jnp.exp(masked - row_peak[..., None]) / row_mass[..., None], 0.0
     ).astype(jnp.bfloat16)
-    weights = lax.all_gather(weights, "width", axis=0, tiled=True)
+    weights = gather_around(weights, "width", 0)
     value_heads = value_rows.reshape(col_count, KV, HD)
     out_cols = out_proj.shape[1]
     proj_heads = out_proj.reshape(-1, HD, out_cols)

time: 432 us -> 367 us (0.85)
  waiting for transfers between devices: 160 us -> 78.2 us
  local copies, waits for them, and re-layouts: 64.2 us -> 73.7 us
    all_gather x1, waiting for transfers between devices: 100 us -> 22.5 us  [body(): portion = lax.all_gather(proj_heads, ('row', 'src'), axis=0, tiled=True)]
    all_gather x1 -> x0, waiting for transfers between devices: 47.7 us -> none  [body(): weights = lax.all_gather(weights, 'width', axis=0, tiled=True)]
    ppermute x0 -> x3, waiting for transfers between devices: none -> 43.3 us  [the longest x2 43.3 us: gather_around(): earlier.append(lax.ppermute(earlier[-1], axis, up))]
    unnamed x6 -> x13, local copies, waits for them, and re-layouts: 1.53 us -> 6.94 us
  transfers between devices with their start and end apart: 4 -> 6, of which waited for: 4 -> 5; matrix products, arithmetic and copies ran while one was open for 4% -> 10% of each run, Pallas kernels for 0% -> 0%
where the time goes in v1:
time: 367 us; the launch traced here: 366 us
  matrix products  123 us (34%)
  waiting for transfers between devices  78.2 us (21%)
  local copies, waits for them, and re-layouts  73.7 us (20%)
  other arithmetic  31.5 us (9%)
  loops' own time  22.2 us (6%)
  starting transfers between devices  14.8 us (4%)
  between operations  13.6 us (4%)
  blocking collectives  8.8 us (2%)
    dot_general x16, matrix products, compute(): jnp.einsum('hij,jhe->ije', attend, source_images, preferred_element_type=...  96.1 us
    while x2, local copies, waits for them, and re-layouts, body(): lax.fori_loop(0, turns, tile, jnp.zeros((row_count, col_count), jnp.float...  45.7 us
    ppermute x2, waiting for transfers between devices, gather_around(): earlier.append(lax.ppermute(earlier[-1], axis, up))  43.3 us
    dot_general x1, matrix products, body(): jnp.einsum('jhd,hde->jhe', chosen, portion, preferred_element_type=jnp.fl...  24.2 us
    all_gather x1, waiting for transfers between devices, body(): portion = lax.all_gather(proj_heads, ('row', 'src'), axis=0, tiled=True)  22.5 us
    another operation x1, loops' own time, body(): lax.fori_loop(0, turns, tile, jnp.zeros((row_count, col_count), jnp.float...  21.8 us
    dynamic_update_slice x16, local copies, waits for them, and re-layouts, tile(): return lax.dynamic_update_slice(running, result, (row_start, col_start))  13.7 us
    reduce_max x16, other arithmetic, tile(): jnp.max(row_slice) >= jnp.min(col_slice)  12.5 us
  transfers between devices with their start and end apart: 6, of which 5 were waited for; matrix products, arithmetic and copies ran while one was open for 10% of the time, Pallas kernels for 0%

profile of v1, /device:TPU:25, one launch (start us, length us, event | category | flops | bytes accessed | tf_op | source)
XLA Modules:
  0.0 365.7 jit_solution(11068839865914366792)
XLA Ops:
  7.3 1.4 copy.36
  10.9 5.0 %all-to-all-start = ((f32[8,32,256]{2,1,0:T(8,128)}), f32[8,32,256]{2,1,0:T(8,128)S(1)}, u32[]{:S(2)}, u32[]{:S(2)}) async-start(f32[8,32,256]{2,1,0:T(8,128)} %broadcast_in_dim.44), calls=%async_computation | async-start | bytes 524288 | tf_op jit(solution)/shard_map/all_to_all | solution.py:27
  16.0 1.9 copy.27
  17.9 4.4 %all-to-all-done = f32[8,32,256]{2,1,0:T(8,128)S(1)} async-done(((f32[8,32,256]{2,1,0:T(8,128)}), f32[8,32,256]{2,1,0:T(8,128)S(1)}, u32[]{:S(2)}, u32[]{:S(2)}) %all-to-all-start) | async-done | bytes 262176 | tf_op jit(solution)/shard_map/all_to_all | solution.py:27
  22.5 2.1 select_convert_fusion
  24.5 1.6 collective-permute-start
  26.2 24.8 %collective-permute-done = bf16[16,256,128]{2,1,0:T(8,128)(2,1)S(1)} collective-permute-done((bf16[16,256,128]{2,1,0:T(8,128)(2,1)}, bf16[16,256,128]{2,1,0:T(8,128)(2,1)S(1)}, u32[]{:S(2)}, u32[]{:S(2)}) %collective-permute-start) | collective-permute-done | bytes 1048608 | tf_op jit(solution)/shard_map/ppermute | solution.py:18
  51.0 2.7 collective-permute-start.2
  53.7 1.1 copy.35
  54.7 2.0 convert_bitcast_fusion.1
  56.8 18.5 %collective-permute-done.1 = bf16[16,256,128]{2,1,0:T(8,128)(2,1)} collective-permute-done((bf16[16,256,128]{2,1,0:T(8,128)(2,1)S(1)}, bf16[16,256,128]{2,1,0:T(8,128)(2,1)}, u32[]{:S(2)}, u32[]{:S(2)}) %collective-permute-start.1) | collective-permute-done | bytes 1048608 | tf_op jit(solution)/shard_map/ppermute | solution.py:18
  75.3 1.3 constant_dynamic-update-slice_fusion.7
  76.7 1.7 constant_dynamic-update-slice_fusion.5
  78.4 1.4 constant_dynamic-update-slice_fusion.4
  79.9 1.4 constant_dynamic-update-slice_fusion.3
  81.4 1.7 constant_dynamic-update-slice_fusion.1
  83.1 1.4 constant_dynamic-update-slice_fusion
  84.5 2.3 constant_dynamic-slice_fusion
  86.9 15.8 %copy.29 = bf16[64,256,128]{0,1,2:T(8,128)(2,1)} copy(bf16[64,256,128]{2,1,0:T(8,128)(2,1)} %constant_dynamic-slice_fusion) | data formatting | bytes 8388608 | tf_op jit(solution)/shard_map/while | solution.py:148
  102.6 22.5 %all-gather.2.cloned.1.call-done = bf16[64,128,2048]{2,1,0:T(8,128)(2,1)} async-done(((bf16[2,128,2048]{2,1,0:T(8,128)(2,1)}), bf16[64,128,2048]{2,1,0:T(8,128)(2,1)}) %all-gather.2.cloned.1.call-update) | async-done | bytes 33554448 | tf_op jit(solution)/shard_map/all_gather | solution.py:109
  125.1 24.2 %convert_bitcast_fusion = bf16[128,64,2048]{2,0,1:T(8,128)(2,1)} fusion(bf16[64,128,2048]{2,1,0:T(8,128)(2,1)} %all-gather.2.cloned.1.call-done, bf16[128,64,128]{2,1,0:T(8,128)(2,1)S(1)} %copy-done.1), kind=kOutput, calls=%fused_computation.7 | convolution fusion | flops 4311744512 | bytes 69206016 | tf_op jit(solution)/shard_map/jhd,hde->jhe/dot_general | solution.py:118
  149.3 30.0 %copy.28 = bf16[128,64,2048]{2,1,0:T(8,128)(2,1)} copy(bf16[128,64,2048]{2,0,1:T(8,128)(2,1)} %convert_bitcast_fusion) | data formatting | bytes 67108864 | tf_op jit(solution)/shard_map/while | solution.py:148
  179.3 156.7 %while.15 = (s32[]{:T(128)}, f32[256,128]{0,1:T(8,128)S(1)}, s32[256]{0:T(256)S(1)}, s32[128]{0:T(128)S(1)}, bf16[128,64,2048]{2,1,0:T(8,128)(2,1)}, /*index=5*/...) while((s32[]{:T(128)}, f32[256,128]{0,1:T(8,128)S(1)}, ...), condition=%wide.region_8.9_spmd, body=%wide.region_2.8_spmd.sunk | while | flops 545257600 | bytes 8939898 | solution.py:148
  182.2 6.0 %conditional.2 = (f32[64,32]{0,1:T(8,128)S(1)}) conditional(s32[]{:T(128)} %convert_element_type.48, () %tuple.54, (s32[]{:T(128)}, bf16[128,64,2048]{2,1,0:T(8,128)(2,1)}, s32[]{:T(128)}, bf16[64,256,128]{0,1,2:T(8,128)(2,1)}) %tuple.55), branch_computations={%region_5.5_spmd, %region_6.7_spmd} | conditional | flops 545257472 | bytes 8922700 | solution.py:145
  182.2 6.0 %abs_reduce_fusion = f32[32,64]{1,0:T(8,128)S(1)} fusion(bf16[128,64,2048]{2,1,0:T(8,128)(2,1)} %get-tuple-element.172, s32[]{:T(128)S(6)} %select_n.87, bf16[64,256,128]{0,1,2:T(8,128)(2,1)} %get-tuple-element.174, s32[]{:T(128)S(6)} %select_n.88), kind=kOutput, calls=%fused_computation | convolution fusion | flops 545257472 | bytes 8922624 | tf_op jit(solution)/shard_map/while/body/eval_jaxpr/cond/branch_1_fun/hij,jhe->ije/dot_general | solution.py:137
  192.0 6.0 %conditional.2 = (f32[64,32]{0,1:T(8,128)S(1)}) conditional(s32[]{:T(128)} %convert_element_type.48, () %tuple.54, (s32[]{:T(128)}, bf16[128,64,2048]{2,1,0:T(8,128)(2,1)}, s32[]{:T(128)}, bf16[64,256,128]{0,1,2:T(8,128)(2,1)}) %tuple.55), branch_computations={%region_5.5_spmd, %region_6.7_spmd} | conditional | flops 545257472 | bytes 8922700 | solution.py:145
  192.0 6.0 %abs_reduce_fusion = f32[32,64]{1,0:T(8,128)S(1)} fusion(bf16[128,64,2048]{2,1,0:T(8,128)(2,1)} %get-tuple-element.172, s32[]{:T(128)S(6)} %select_n.87, bf16[64,256,128]{0,1,2:T(8,128)(2,1)} %get-tuple-element.174, s32[]{:T(128)S(6)} %select_n.88), kind=kOutput, calls=%fused_computation | convolution fusion | flops 545257472 | bytes 8922624 | tf_op jit(solution)/shard_map/while/body/eval_jaxpr/cond/branch_1_fun/hij,jhe->ije/dot_general | solution.py:137
  201.8 6.0 %conditional.2 = (f32[64,32]{0,1:T(8,128)S(1)}) conditional(s32[]{:T(128)} %convert_element_type.48, () %tuple.54, (s32[]{:T(128)}, bf16[128,64,2048]{2,1,0:T(8,128)(2,1)}, s32[]{:T(128)}, bf16[64,256,128]{0,1,2:T(8,128)(2,1)}) %tuple.55), branch_computations={%region_5.5_spmd, %region_6.7_spmd} | conditional | flops 545257472 | bytes 8922700 | solution.py:145
  201.8 6.0 %abs_reduce_fusion = f32[32,64]{1,0:T(8,128)S(1)} fusion(bf16[128,64,2048]{2,1,0:T(8,128)(2,1)} %get-tuple-element.172, s32[]{:T(128)S(6)} %select_n.87, bf16[64,256,128]{0,1,2:T(8,128)(2,1)} %get-tuple-element.174, s32[]{:T(128)S(6)} %select_n.88), kind=kOutput, calls=%fused_computation | convolution fusion | flops 545257472 | bytes 8922624 | tf_op jit(solution)/shard_map/while/body/eval_jaxpr/cond/branch_1_fun/hij,jhe->ije/dot_general | solution.py:137
  211.6 6.0 %conditional.2 = (f32[64,32]{0,1:T(8,128)S(1)}) conditional(s32[]{:T(128)} %convert_element_type.48, () %tuple.54, (s32[]{:T(128)}, bf16[128,64,2048]{2,1,0:T(8,128)(2,1)}, s32[]{:T(128)}, bf16[64,256,128]{0,1,2:T(8,128)(2,1)}) %tuple.55), branch_computations={%region_5.5_spmd, %region_6.7_spmd} | conditional | flops 545257472 | bytes 8922700 | solution.py:145
  211.6 6.0 %abs_reduce_fusion = f32[32,64]{1,0:T(8,128)S(1)} fusion(bf16[128,64,2048]{2,1,0:T(8,128)(2,1)} %get-tuple-element.172, s32[]{:T(128)S(6)} %select_n.87, bf16[64,256,128]{0,1,2:T(8,128)(2,1)} %get-tuple-element.174, s32[]{:T(128)S(6)} %select_n.88), kind=kOutput, calls=%fused_computation | convolution fusion | flops 545257472 | bytes 8922624 | tf_op jit(solution)/shard_map/while/body/eval_jaxpr/cond/branch_1_fun/hij,jhe->ije/dot_general | solution.py:137
  221.2 6.0 %conditional.2 = (f32[64,32]{0,1:T(8,128)S(1)}) conditional(s32[]{:T(128)} %convert_element_type.48, () %tuple.54, (s32[]{:T(128)}, bf16[128,64,2048]{2,1,0:T(8,128)(2,1)}, s32[]{:T(128)}, bf16[64,256,128]{0,1,2:T(8,128)(2,1)}) %tuple.55), branch_computations={%region_5.5_spmd, %region_6.7_spmd} | conditional | flops 545257472 | bytes 8922700 | solution.py:145
  221.2 6.0 %abs_reduce_fusion = f32[32,64]{1,0:T(8,128)S(1)} fusion(bf16[128,64,2048]{2,1,0:T(8,128)(2,1)} %get-tuple-element.172, s32[]{:T(128)S(6)} %select_n.87, bf16[64,256,128]{0,1,2:T(8,128)(2,1)} %get-tuple-element.174, s32[]{:T(128)S(6)} %select_n.88), kind=kOutput, calls=%fused_computation | convolution fusion | flops 545257472 | bytes 8922624 | tf_op jit(solution)/shard_map/while/body/eval_jaxpr/cond/branch_1_fun/hij,jhe->ije/dot_general | solution.py:137
  227.2 1.1 dynamic_update_slice.11
  231.2 6.0 %conditional.2 = (f32[64,32]{0,1:T(8,128)S(1)}) conditional(s32[]{:T(128)} %convert_element_type.48, () %tuple.54, (s32[]{:T(128)}, bf16[128,64,2048]{2,1,0:T(8,128)(2,1)}, s32[]{:T(128)}, bf16[64,256,128]{0,1,2:T(8,128)(2,1)}) %tuple.55), branch_computations={%region_5.5_spmd, %region_6.7_spmd} | conditional | flops 545257472 | bytes 8922700 | solution.py:145
  231.3 6.0 %abs_reduce_fusion = f32[32,64]{1,0:T(8,128)S(1)} fusion(bf16[128,64,2048]{2,1,0:T(8,128)(2,1)} %get-tuple-element.172, s32[]{:T(128)S(6)} %select_n.87, bf16[64,256,128]{0,1,2:T(8,128)(2,1)} %get-tuple-element.174, s32[]{:T(128)S(6)} %select_n.88), kind=kOutput, calls=%fused_computation | convolution fusion | flops 545257472 | bytes 8922624 | tf_op jit(solution)/shard_map/while/body/eval_jaxpr/cond/branch_1_fun/hij,jhe->ije/dot_general | solution.py:137
  237.3 1.1 dynamic_update_slice.11
  241.3 6.0 %conditional.2 = (f32[64,32]{0,1:T(8,128)S(1)}) conditional(s32[]{:T(128)} %convert_element_type.48, () %tuple.54, (s32[]{:T(128)}, bf16[128,64,2048]{2,1,0:T(8,128)(2,1)}, s32[]{:T(128)}, bf16[64,256,128]{0,1,2:T(8,128)(2,1)}) %tuple.55), branch_computations={%region_5.5_spmd, %region_6.7_spmd} | conditional | flops 545257472 | bytes 8922700 | solution.py:145
  241.3 6.0 %abs_reduce_fusion = f32[32,64]{1,0:T(8,128)S(1)} fusion(bf16[128,64,2048]{2,1,0:T(8,128)(2,1)} %get-tuple-element.172, s32[]{:T(128)S(6)} %select_n.87, bf16[64,256,128]{0,1,2:T(8,128)(2,1)} %get-tuple-element.174, s32[]{:T(128)S(6)} %select_n.88), kind=kOutput, calls=%fused_computation | convolution fusion | flops 545257472 | bytes 8922624 | tf_op jit(solution)/shard_map/while/body/eval_jaxpr/cond/branch_1_fun/hij,jhe->ije/dot_general | solution.py:137
  247.4 1.1 dynamic_update_slice.11
  251.4 6.0 %conditional.2 = (f32[64,32]{0,1:T(8,128)S(1)}) conditional(s32[]{:T(128)} %convert_element_type.48, () %tuple.54, (s32[]{:T(128)}, bf16[128,64,2048]{2,1,0:T(8,128)(2,1)}, s32[]{:T(128)}, bf16[64,256,128]{0,1,2:T(8,128)(2,1)}) %tuple.55), branch_computations={%region_5.5_spmd, %region_6.7_spmd} | conditional | flops 545257472 | bytes 8922700 | solution.py:145
  251.4 6.0 %abs_reduce_fusion = f32[32,64]{1,0:T(8,128)S(1)} fusion(bf16[128,64,2048]{2,1,0:T(8,128)(2,1)} %get-tuple-element.172, s32[]{:T(128)S(6)} %select_n.87, bf16[64,256,128]{0,1,2:T(8,128)(2,1)} %get-tuple-element.174, s32[]{:T(128)S(6)} %select_n.88), kind=kOutput, calls=%fused_computation | convolution fusion | flops 545257472 | bytes 8922624 | tf_op jit(solution)/shard_map/while/body/eval_jaxpr/cond/branch_1_fun/hij,jhe->ije/dot_general | solution.py:137
  257.4 0.9 dynamic_update_slice.11
  261.3 6.0 %conditional.2 = (f32[64,32]{0,1:T(8,128)S(1)}) conditional(s32[]{:T(128)} %convert_element_type.48, () %tuple.54, (s32[]{:T(128)}, bf16[128,64,2048]{2,1,0:T(8,128)(2,1)}, s32[]{:T(128)}, bf16[64,256,128]{0,1,2:T(8,128)(2,1)}) %tuple.55), branch_computations={%region_5.5_spmd, %region_6.7_spmd} | conditional | flops 545257472 | bytes 8922700 | solution.py:145
  261.3 6.0 %abs_reduce_fusion = f32[32,64]{1,0:T(8,128)S(1)} fusion(bf16[128,64,2048]{2,1,0:T(8,128)(2,1)} %get-tuple-element.172, s32[]{:T(128)S(6)} %select_n.87, bf16[64,256,128]{0,1,2:T(8,128)(2,1)} %get-tuple-element.174, s32[]{:T(128)S(6)} %select_n.88), kind=kOutput, calls=%fused_computation | convolution fusion | flops 545257472 | bytes 8922624 | tf_op jit(solution)/shard_map/while/body/eval_jaxpr/cond/branch_1_fun/hij,jhe->ije/dot_general | solution.py:137
  270.9 6.0 %conditional.2 = (f32[64,32]{0,1:T(8,128)S(1)}) conditional(s32[]{:T(128)} %convert_element_type.48, () %tuple.54, (s32[]{:T(128)}, bf16[128,64,2048]{2,1,0:T(8,128)(2,1)}, s32[]{:T(128)}, bf16[64,256,128]{0,1,2:T(8,128)(2,1)}) %tuple.55), branch_computations={%region_5.5_spmd, %region_6.7_spmd} | conditional | flops 545257472 | bytes 8922700 | solution.py:145
  270.9 6.0 %abs_reduce_fusion = f32[32,64]{1,0:T(8,128)S(1)} fusion(bf16[128,64,2048]{2,1,0:T(8,128)(2,1)} %get-tuple-element.172, s32[]{:T(128)S(6)} %select_n.87, bf16[64,256,128]{0,1,2:T(8,128)(2,1)} %get-tuple-element.174, s32[]{:T(128)S(6)} %select_n.88), kind=kOutput, calls=%fused_computation | convolution fusion | flops 545257472 | bytes 8922624 | tf_op jit(solution)/shard_map/while/body/eval_jaxpr/cond/branch_1_fun/hij,jhe->ije/dot_general | solution.py:137
  280.4 6.0 %conditional.2 = (f32[64,32]{0,1:T(8,128)S(1)}) conditional(s32[]{:T(128)} %convert_element_type.48, () %tuple.54, (s32[]{:T(128)}, bf16[128,64,2048]{2,1,0:T(8,128)(2,1)}, s32[]{:T(128)}, bf16[64,256,128]{0,1,2:T(8,128)(2,1)}) %tuple.55), branch_computations={%region_5.5_spmd, %region_6.7_spmd} | conditional | flops 545257472 | bytes 8922700 | solution.py:145
  280.5 6.0 %abs_reduce_fusion = f32[32,64]{1,0:T(8,128)S(1)} fusion(bf16[128,64,2048]{2,1,0:T(8,128)(2,1)} %get-tuple-element.172, s32[]{:T(128)S(6)} %select_n.87, bf16[64,256,128]{0,1,2:T(8,128)(2,1)} %get-tuple-element.174, s32[]{:T(128)S(6)} %select_n.88), kind=kOutput, calls=%fused_computation | convolution fusion | flops 545257472 | bytes 8922624 | tf_op jit(solution)/shard_map/while/body/eval_jaxpr/cond/branch_1_fun/hij,jhe->ije/dot_general | solution.py:137
  290.0 6.0 %conditional.2 = (f32[64,32]{0,1:T(8,128)S(1)}) conditional(s32[]{:T(128)} %convert_element_type.48, () %tuple.54, (s32[]{:T(128)}, bf16[128,64,2048]{2,1,0:T(8,128)(2,1)}, s32[]{:T(128)}, bf16[64,256,128]{0,1,2:T(8,128)(2,1)}) %tuple.55), branch_computations={%region_5.5_spmd, %region_6.7_spmd} | conditional | flops 545257472 | bytes 8922700 | solution.py:145
  290.1 6.0 %abs_reduce_fusion = f32[32,64]{1,0:T(8,128)S(1)} fusion(bf16[128,64,2048]{2,1,0:T(8,128)(2,1)} %get-tuple-element.172, s32[]{:T(128)S(6)} %select_n.87, bf16[64,256,128]{0,1,2:T(8,128)(2,1)} %get-tuple-element.174, s32[]{:T(128)S(6)} %select_n.88), kind=kOutput, calls=%fused_computation | convolution fusion | flops 545257472 | bytes 8922624 | tf_op jit(solution)/shard_map/while/body/eval_jaxpr/cond/branch_1_fun/hij,jhe->ije/dot_general | solution.py:137
  299.5 6.0 %conditional.2 = (f32[64,32]{0,1:T(8,128)S(1)}) conditional(s32[]{:T(128)} %convert_element_type.48, () %tuple.54, (s32[]{:T(128)}, bf16[128,64,2048]{2,1,0:T(8,128)(2,1)}, s32[]{:T(128)}, bf16[64,256,128]{0,1,2:T(8,128)(2,1)}) %tuple.55), branch_computations={%region_5.5_spmd, %region_6.7_spmd} | conditional | flops 545257472 | bytes 8922700 | solution.py:145
  299.5 6.0 %abs_reduce_fusion = f32[32,64]{1,0:T(8,128)S(1)} fusion(bf16[128,64,2048]{2,1,0:T(8,128)(2,1)} %get-tuple-element.172, s32[]{:T(128)S(6)} %select_n.87, bf16[64,256,128]{0,1,2:T(8,128)(2,1)} %get-tuple-element.174, s32[]{:T(128)S(6)} %select_n.88), kind=kOutput, calls=%fused_computation | convolution fusion | flops 545257472 | bytes 8922624 | tf_op jit(solution)/shard_map/while/body/eval_jaxpr/cond/branch_1_fun/hij,jhe->ije/dot_general | solution.py:137
  305.5 0.9 dynamic_update_slice.11
  309.4 6.0 %conditional.2 = (f32[64,32]{0,1:T(8,128)S(1)}) conditional(s32[]{:T(128)} %convert_element_type.48, () %tuple.54, (s32[]{:T(128)}, bf16[128,64,2048]{2,1,0:T(8,128)(2,1)}, s32[]{:T(128)}, bf16[64,256,128]{0,1,2:T(8,128)(2,1)}) %tuple.55), branch_computations={%region_5.5_spmd, %region_6.7_spmd} | conditional | flops 545257472 | bytes 8922700 | solution.py:145
  309.4 6.0 %abs_reduce_fusion = f32[32,64]{1,0:T(8,128)S(1)} fusion(bf16[128,64,2048]{2,1,0:T(8,128)(2,1)} %get-tuple-element.172, s32[]{:T(128)S(6)} %select_n.87, bf16[64,256,128]{0,1,2:T(8,128)(2,1)} %get-tuple-element.174, s32[]{:T(128)S(6)} %select_n.88), kind=kOutput, calls=%fused_computation | convolution fusion | flops 545257472 | bytes 8922624 | tf_op jit(solution)/shard_map/while/body/eval_jaxpr/cond/branch_1_fun/hij,jhe->ije/dot_general | solution.py:137
  315.4 0.9 dynamic_update_slice.11
  319.2 6.0 %conditional.2 = (f32[64,32]{0,1:T(8,128)S(1)}) conditional(s32[]{:T(128)} %convert_element_type.48, () %tuple.54, (s32[]{:T(128)}, bf16[128,64,2048]{2,1,0:T(8,128)(2,1)}, s32[]{:T(128)}, bf16[64,256,128]{0,1,2:T(8,128)(2,1)}) %tuple.55), branch_computations={%region_5.5_spmd, %region_6.7_spmd} | conditional | flops 545257472 | bytes 8922700 | solution.py:145
  319.2 6.0 %abs_reduce_fusion = f32[32,64]{1,0:T(8,128)S(1)} fusion(bf16[128,64,2048]{2,1,0:T(8,128)(2,1)} %get-tuple-element.172, s32[]{:T(128)S(6)} %select_n.87, bf16[64,256,128]{0,1,2:T(8,128)(2,1)} %get-tuple-element.174, s32[]{:T(128)S(6)} %select_n.88), kind=kOutput, calls=%fused_computation | convolution fusion | flops 545257472 | bytes 8922624 | tf_op jit(solution)/shard_map/while/body/eval_jaxpr/cond/branch_1_fun/hij,jhe->ije/dot_general | solution.py:137
  329.1 6.0 %conditional.2 = (f32[64,32]{0,1:T(8,128)S(1)}) conditional(s32[]{:T(128)} %convert_element_type.48, () %tuple.54, (s32[]{:T(128)}, bf16[128,64,2048]{2,1,0:T(8,128)(2,1)}, s32[]{:T(128)}, bf16[64,256,128]{0,1,2:T(8,128)(2,1)}) %tuple.55), branch_computations={%region_5.5_spmd, %region_6.7_spmd} | conditional | flops 545257472 | bytes 8922700 | solution.py:145
  329.1 6.0 %abs_reduce_fusion = f32[32,64]{1,0:T(8,128)S(1)} fusion(bf16[128,64,2048]{2,1,0:T(8,128)(2,1)} %get-tuple-element.172, s32[]{:T(128)S(6)} %select_n.87, bf16[64,256,128]{0,1,2:T(8,128)(2,1)} %get-tuple-element.174, s32[]{:T(128)S(6)} %select_n.88), kind=kOutput, calls=%fused_computation | convolution fusion | flops 545257472 | bytes 8922624 | tf_op jit(solution)/shard_map/while/body/eval_jaxpr/cond/branch_1_fun/hij,jhe->ije/dot_general | solution.py:137
  335.9 8.8 %all_to_all.16 = f32[4,256,32]{1,2,0:T(8,128)S(1)} all-to-all(f32[4,256,32]{1,2,0:T(8,128)S(1)} %bitcast.40), channel_id=1, replica_groups=mesh['width'=4,'row'=4,'src'=8] {'width'}, dimensions={0} | all-to-all | bytes 262144 | tf_op jit(solution)/shard_map/all_to_all | solution.py:68
  345.4 5.5 %all-to-all-start.2 = ((f32[32,1,256]{2,1,0:T(1,128)}), f32[32,1,256]{2,1,0:T(1,128)S(1)}, u32[]{:S(2)}, u32[]{:S(2)}) async-start(f32[32,1,256]{2,1,0:T(1,128)} %broadcast_in_dim.46), calls=%async_computation.2 | async-start | bytes 65536 | tf_op jit(solution)/shard_map/all_to_all | solution.py:27
  351.0 7.2 %all-to-all-done.2 = f32[32,1,256]{2,1,0:T(1,128)S(1)} async-done(((f32[32,1,256]{2,1,0:T(1,128)}), f32[32,1,256]{2,1,0:T(1,128)S(1)}, u32[]{:S(2)}, u32[]{:S(2)}) %all-to-all-start.2) | async-done | bytes 32800 | tf_op jit(solution)/shard_map/all_to_all | solution.py:27
  (74 shorter events, 36.9 us)
Async XLA Ops:
  6.5 2.2 copy-start.2
  6.5 118.6 %all-gather.2.cloned.1.call-start = ((), (), s32[]{:S(2)}) async-start(), calls=%async_computation.3 | async-start | bytes 34603008 | tf_op jit(solution)/shard_map/all_gather | solution.py:109
  9.5 6.5 %copy-start = (f32[2,128,256,8]{2,1,3,0:T(8,128)}, f32[2,128,256,8]{2,1,3,0:T(8,128)S(1)}, u32[]{:S(2)}) copy-start(f32[2,128,256,8]{2,1,3,0:T(8,128)S(1)} %get-tuple-element.232) | copy-start | bytes 6291460
  10.9 11.5 %all-to-all-start = ((f32[8,32,256]{2,1,0:T(8,128)}), f32[8,32,256]{2,1,0:T(8,128)S(1)}, u32[]{:S(2)}, u32[]{:S(2)}) async-start(f32[8,32,256]{2,1,0:T(8,128)} %broadcast_in_dim.44), calls=%async_computation | async-start | bytes 524288 | tf_op jit(solution)/shard_map/all_to_all | solution.py:27
  24.5 26.4 %collective-permute-start = (bf16[16,256,128]{2,1,0:T(8,128)(2,1)}, bf16[16,256,128]{2,1,0:T(8,128)(2,1)S(1)}, u32[]{:S(2)}, u32[]{:S(2)}) collective-permute-start(bf16[16,256,128]{2,1,0:T(8,128)(2,1)} %select_convert_fusion), channel_id=1, source_target_pairs={{0,32},{32,64},{64,96},{96,0},{1,33},{33,65},{65,97},{97,1},{2,34}... | collective-permute-start | bytes 3145736 | tf_op jit(solution)/shard_map/ppermute | solution.py:18
  51.0 24.3 %collective-permute-start.1 = (bf16[16,256,128]{2,1,0:T(8,128)(2,1)S(1)}, bf16[16,256,128]{2,1,0:T(8,128)(2,1)}, u32[]{:S(2)}, u32[]{:S(2)}) collective-permute-start(bf16[16,256,128]{2,1,0:T(8,128)(2,1)S(1)} %collective-permute-done), channel_id=1, source_target_pairs={{0,32},{32,64},{64,96},{96,0},{1,33},{33,65},{65,97},{97,1},{2,34}... | collective-permute-start | bytes 3145736 | tf_op jit(solution)/shard_map/ppermute | solution.py:18
  51.0 27.4 %collective-permute-start.2 = (bf16[16,256,128]{2,1,0:T(8,128)(2,1)}, bf16[16,256,128]{2,1,0:T(8,128)(2,1)}, u32[]{:S(2)}, u32[]{:S(2)}) collective-permute-start(bf16[16,256,128]{2,1,0:T(8,128)(2,1)} %select_convert_fusion), channel_id=1, source_target_pairs={{0,96},{32,0},{64,32},{96,64},{1,97},{33,1},{65,33},{97,65},{2,98}... | collective-permute-start | bytes 3145736 | tf_op jit(solution)/shard_map/ppermute | solution.py:20
  86.9 38.2 %copy-start.1 = (bf16[128,64,128]{2,1,0:T(8,128)(2,1)S(1)}, bf16[128,64,128]{2,1,0:T(8,128)(2,1)}, u32[]{:S(2)}) copy-start(bf16[128,64,128]{2,1,0:T(8,128)(2,1)} %convert_bitcast_fusion.1) | copy-start | bytes 6291460
  345.4 12.8 %all-to-all-start.2 = ((f32[32,1,256]{2,1,0:T(1,128)}), f32[32,1,256]{2,1,0:T(1,128)S(1)}, u32[]{:S(2)}, u32[]{:S(2)}) async-start(f32[32,1,256]{2,1,0:T(1,128)} %broadcast_in_dim.46), calls=%async_computation.2 | async-start | bytes 65536 | tf_op jit(solution)/shard_map/all_to_all | solution.py:27
Sparse Core Ops, SparseCore 0:
  9.6 115.4 all-gather.1
